TPU v7x, 128 devices: a whole 4x4x4 slice. The times are simulated.
128 devices in a mesh: dp: 32 (over z, y, core), col: 4 (over x).
Axes of the slice: x: 4, y: 4, z: 4, core: 2. Of those that a mesh axis runs over, the one named last changes fastest.
Arguments:
- tokens: bfloat16 [32768, 8192], P('dp', 'col'), may hold values from -6 to 6
- out_grad: bfloat16 [32768, 8192], P(('dp', 'col')), may hold values from -24 to 24
- weight: float32 [8192, 8192], P('dp', 'col'), may hold values from -6 to 6
- second: float32 [8192, 8192], P('dp', 'col'), may hold values from 0.0001 to 0.001
- momentum: float32 [8192, 512], P(('dp', 'col')), may hold values from -0.12 to 0.12
- sign_seed: int32 [1], replicated, may hold values from 0 to 999999
- step_number: int32 [1], replicated, may hold values from 1 to 999999
Outputs:
- new_weight: float32 [8192, 8192], P('dp', 'col')
- new_second: float32 [8192, 8192], P('dp', 'col')
- new_momentum: float32 [8192, 512], P(('dp', 'col'))
All inputs are finite; a program needn't handle non-finite values.
Results may differ from a plain program's by a relative error of at most 0.00097.
Values may be sent and summed in bfloat16 or wider, within the bound.
A program may use at most 128 MiB of HBM per device.

v0:
```python
import jax
import jax.numpy as jnp
from jax import lax
from jax.sharding import Mesh
from jax.sharding import PartitionSpec as P

DP = ("dp_0", "dp_1", "dp_2")
DP_COL = ("dp_0", "dp_1", "dp_2", "col")


def split_up(x, dim, count):
    before, after = (x.shape[:dim], x.shape[dim + 1 :])
    return jnp.moveaxis(x.reshape(*before, count, -1, *after), dim, 0)


def sent_and_summed(x, axis, dim):
    count = lax.axis_size(axis)
    pieces = lax.all_to_all(split_up(x, dim, count), axis, 0, 0, tiled=True)
    return jnp.sum(pieces, axis=0)


def from_everyone(x, axis):
    copies = jnp.broadcast_to(x, (lax.axis_size(axis), *x.shape))
    return lax.all_to_all(copies, axis, split_axis=0, concat_axis=0, tiled=True)


def joined_along(pieces, dim):
    pieces = jnp.moveaxis(pieces, 0, dim)
    lengths = pieces.shape
    return pieces.reshape(*lengths[:dim], lengths[dim] * lengths[dim + 1], *lengths[dim + 2 :])


def gather_directly(x, axis, dim):
    pieces = from_everyone(x, axis)
    return joined_along(pieces, dim)


def sum_in_two_steps(x, axes, dim):
    far, near = axes
    own = sent_and_summed(split_up(x, dim, lax.axis_size(far)), near, dim + 1)
    return jnp.sum(lax.all_to_all(own, far, 0, 0, tiled=True), axis=0)


def sign_table(sign_seed, step_number, first_row, row_count, low_rank):
    row_ids = first_row + lax.iota(jnp.int32, row_count)
    col_ids = lax.iota(jnp.int32, low_rank)
    flat_index = row_ids[:, None] * low_rank + col_ids[None, :]
    hashed = flat_index * 747796405 + sign_seed[0] * 1664525 + step_number[0] * 1013904223
    hashed = hashed ^ hashed >> 16 & 65535
    hashed = hashed * 2127912213
    hashed = hashed ^ hashed >> 13 & 524287
    hashed = hashed * 1103515245
    hashed = hashed ^ hashed >> 16 & 65535
    low_bit = hashed >> 20 & 1
    return (1 - 2 * low_bit).astype(jnp.float32)


def contract(left_rows, right_rows):
    return lax.dot_general(
        left_rows, right_rows, (((0,), (0,)), ((), ())), preferred_element_type=jnp.float32
    )


def per_device(tokens, out_grad, weight, second, momentum, sign_seed, step_number):
    local_tokens, din_local = tokens.shape
    low_rank = momentum.shape[1]
    owner_rows = momentum.shape[0]
    inv_root = 1.0 / jnp.sqrt(jnp.float32(low_rank))
    col_position = lax.axis_index("col")
    sign_block = sign_table(sign_seed, step_number, col_position * din_local, din_local, low_rank)
    partial_sketch = (
        jnp.dot(tokens, sign_block.astype(jnp.bfloat16), preferred_element_type=jnp.float32)
        * inv_root
    )
    quarter = sent_and_summed(partial_sketch, "col", 0)
    sketch = quarter.astype(jnp.bfloat16)
    total_tokens = lax.axis_size(DP) * local_tokens
    data_count = lax.axis_size(DP)
    col_count = lax.axis_size("col")
    quarter_rows = out_grad.shape[0]
    grouped = out_grad.reshape(quarter_rows, data_count, col_count, owner_rows)
    grouped = jnp.transpose(grouped, (0, 2, 1, 3)).reshape(
        quarter_rows, col_count, data_count * owner_rows
    )
    regrouped = lax.all_to_all(grouped, "col", split_axis=1, concat_axis=0, tiled=True)
    regrouped = regrouped.reshape(quarter_rows * col_count, data_count * owner_rows)
    shard_sketch = gather_directly(sketch, "col", 0)
    projected = sum_in_two_steps(contract(regrouped, shard_sketch), (("dp_0", "dp_1"), "dp_2"), 0)
    projected = projected / jnp.float32(total_tokens)
    new_momentum = 0.8 * momentum + 0.2 * projected
    row_block = gather_directly(new_momentum, "col", 0)
    dense_grad = (
        lax.dot_general(
            row_block,
            sign_block,
            (((1,), (1,)), ((), ())),
            precision=lax.Precision.HIGHEST,
            preferred_element_type=jnp.float32,
        )
        * inv_root
    )
    new_second = 0.95 * second + 0.05 * dense_grad * dense_grad
    new_weight = weight - 0.5 * dense_grad / (jnp.sqrt(new_second) + 1e-08)
    return (new_weight, new_second, new_momentum)


def solution(mesh):
    torus = Mesh(mesh.devices.reshape(4, 4, 2, mesh.shape["col"]), ("dp_0", "dp_1", "dp_2", "col"))
    return jax.shard_map(
        per_device,
        mesh=torus,
        in_specs=(
            P(DP, "col"),
            P(DP_COL, None),
            P(DP, "col"),
            P(DP, "col"),
            P(DP_COL, None),
            P(),
            P(),
        ),
        out_specs=(P(DP, "col"), P(DP, "col"), P(DP_COL, None)),
        check_vma=False,
    )
```

profile of v0, /device:TPU:0, one launch (start us, length us, event | category | flops | bytes accessed | tf_op | source)
XLA Modules:
  0.0 196.9 jit_solution(12246148960320195151)
XLA Ops:
  1.9 6.4 %fusion.3 = f32[512,1024]{1,0:T(8,128)S(1)} fusion(bf16[1024,2048]{1,0:T(8,128)(2,1)} %param.7, s32[]{:T(128)} %bitcast.1, s32[]{:T(128)} %bitcast, s32[2048]{0:T(1024)S(1)} %add_multiply_fusion), kind=kOutput, calls=%fused_computation.9 | convolution fusion | flops 2170028032 | bytes 6299656 | tf_op jit(solution)/shard_map/dot_general | solution.py:72
  8.3 1.5 copy.33
  9.8 4.4 %all-to-all-start = ((f32[4,256,512]{1,2,0:T(8,128)}), f32[4,256,512]{1,2,0:T(8,128)S(1)}, u32[]{:S(2)}, u32[]{:S(2)}) async-start(f32[4,256,512]{1,2,0:T(8,128)} %bitcast.30), calls=%async_computation | async-start | bytes 4194304 | tf_op jit(solution)/shard_map/all_to_all | solution.py:18
  14.2 6.4 %copy.25 = bf16[256,8192]{0,1:T(8,128)(2,1)} copy(bf16[256,8192]{1,0:T(8,128)(2,1)} %param.8) | data formatting | bytes 8388608 | tf_op args[1]
  20.6 4.7 %copy.26 = bf16[256,4,32,64]{0,3,2,1:T(8,128)(2,1)} copy(bf16[256,4,32,64]{0,3,1,2:T(8,128)(2,1)} %bitcast.29) | data formatting | bytes 8388608 | tf_op jit(solution)/shard_map/transpose | solution.py:82
  25.3 15.2 %all-to-all-done = f32[4,256,512]{1,2,0:T(8,128)S(1)} async-done(((f32[4,256,512]{1,2,0:T(8,128)}), f32[4,256,512]{1,2,0:T(8,128)S(1)}, u32[]{:S(2)}, u32[]{:S(2)}) %all-to-all-start) | async-done | bytes 2097184 | tf_op jit(solution)/shard_map/all_to_all | solution.py:18
  40.5 4.9 %all-to-all-start.2 = ((bf16[256,4,2048]{0,2,1:T(8,128)(2,1)}), bf16[256,4,2048]{0,2,1:T(8,128)(2,1)}, u32[]{:S(2)}, u32[]{:S(2)}) async-start(bf16[256,4,2048]{0,2,1:T(8,128)(2,1)} %bitcast.27), calls=%async_computation.2 | async-start | bytes 8388608 | tf_op jit(solution)/shard_map/all_to_all | solution.py:85
  45.4 0.1 reduce_sum.27
  45.5 0.1 copy.24
  45.7 47.6 %all-to-all-done.2 = bf16[256,4,2048]{0,2,1:T(8,128)(2,1)} async-done(((bf16[256,4,2048]{0,2,1:T(8,128)(2,1)}), bf16[256,4,2048]{0,2,1:T(8,128)(2,1)}, u32[]{:S(2)}, u32[]{:S(2)}) %all-to-all-start.2) | async-done | bytes 4194336 | tf_op jit(solution)/shard_map/all_to_all | solution.py:85
  93.3 1.1 broadcast_in_dim.8
  94.4 3.5 %all-to-all-start.1 = ((bf16[4,256,512]{2,1,0:T(8,128)(2,1)}), bf16[4,256,512]{2,1,0:T(8,128)(2,1)S(1)}, u32[]{:S(2)}, u32[]{:S(2)}) async-start(bf16[4,256,512]{2,1,0:T(8,128)(2,1)} %broadcast_in_dim.8), calls=%async_computation.1 | async-start | bytes 2097152 | tf_op jit(solution)/shard_map/all_to_all | solution.py:24
  97.9 6.3 %copy.27 = bf16[4,256,1,2048]{3,1,0,2:T(8,128)(2,1)} copy(bf16[4,256,1,2048]{1,3,0,2:T(8,128)(2,1)} %bitcast.8) | data formatting | bytes 8388608 | tf_op jit(solution)/shard_map/all_to_all | solution.py:85
  104.2 7.0 %all-to-all-done.1 = bf16[4,256,512]{2,1,0:T(8,128)(2,1)S(1)} async-done(((bf16[4,256,512]{2,1,0:T(8,128)(2,1)}), bf16[4,256,512]{2,1,0:T(8,128)(2,1)S(1)}, u32[]{:S(2)}, u32[]{:S(2)}) %all-to-all-start.1) | async-done | bytes 1048608 | tf_op jit(solution)/shard_map/all_to_all | solution.py:24
  111.1 6.5 %convolution_bitcast_fusion = f32[2048,512]{0,1:T(8,128)} fusion(bf16[1024,512]{1,0:T(8,128)(2,1)S(1)} %bitcast.31, bf16[1024,2048]{1,0:T(8,128)(2,1)} %bitcast.26), kind=kOutput, calls=%fused_computation.4 | convolution fusion | flops 2147483648 | bytes 9437184 | tf_op jit(solution)/shard_map/dot_general | solution.py:59
  117.6 5.4 %copy.28 = f32[2048,512]{1,0:T(8,128)} copy(f32[2048,512]{0,1:T(8,128)} %convolution_bitcast_fusion) | data formatting | bytes 8388608 | tf_op jit(solution)/shard_map/dot_general | solution.py:59
  123.0 2.8 %copy.29 = f32[2,16,64,512]{3,2,1,0:T(8,128)S(1)} copy(f32[2,16,64,512]{3,2,0,1:T(8,128)} %bitcast.28) | data formatting | bytes 8388608 | tf_op jit(solution)/shard_map/transpose | solution.py:13
  125.8 8.2 %all_to_all.40 = f32[2,16,64,512]{3,2,1,0:T(8,128)} all-to-all(f32[2,16,64,512]{3,2,1,0:T(8,128)S(1)} %copy.29), channel_id=1, replica_groups=mesh['dp_0'=4,'dp_1'=4,'dp_2'=2,'col'=4] {'dp_2'}, dimensions={0} | all-to-all | bytes 8388608 | tf_op jit(solution)/shard_map/all_to_all | solution.py:18
  133.9 2.9 %reduce_sum.28 = f32[16,64,512]{2,1,0:T(8,128)S(1)} reduce(f32[2,16,64,512]{3,2,1,0:T(8,128)} %all_to_all.40, f32[]{:T(128)} %constant.21.clone.1), dimensions={0}, to_apply=%region_1.0 | reduce | flops 524288 | bytes 6291460 | tf_op jit(solution)/shard_map/reduce_sum | solution.py:19
  136.8 0.0 copy-start.1
  136.8 36.8 %all_to_all.41 = f32[16,64,512]{2,1,0:T(8,128)} all-to-all(f32[16,64,512]{2,1,0:T(8,128)S(1)} %reduce_sum.28), channel_id=1, replica_groups=mesh['dp_0'=4,'dp_1'=4,'dp_2'=2,'col'=4] {'dp_0','dp_1'}, dimensions={0} | all-to-all | bytes 4194304 | tf_op jit(solution)/shard_map/all_to_all | solution.py:41
  173.6 1.8 reduce_sum.29
  175.3 0.0 copy-done.1
  175.4 0.0 copy-start
  175.4 0.1 broadcast_in_dim.9
  175.5 11.1 %all_to_all.42 = f32[4,64,512]{2,1,0:T(8,128)S(1)} all-to-all(f32[4,64,512]{2,1,0:T(8,128)S(1)} %broadcast_in_dim.9), channel_id=1, replica_groups=mesh['dp_0'=4,'dp_1'=4,'dp_2'=2,'col'=4] {'col'}, dimensions={0} | all-to-all | bytes 1048576 | tf_op jit(solution)/shard_map/all_to_all | solution.py:24
  186.5 10.4 %divide_subtract_fusion = (f32[256,2048]{1,0:T(8,128)}, f32[256,2048]{1,0:T(8,128)}) fusion(f32[256,2048]{1,0:T(8,128)} %param.9, f32[256,2048]{1,0:T(8,128)} %param.10, f32[256,512]{1,0:T(8,128)S(1)} %bitcast.33, s32[]{:T(128)} %bitcast.1, s32[]{:T(128)} %bitcast, s32[2048]{0:T(1024)S(1)} %add_multiply_fusion), kind=kOutput, calls=%fused_computation.7 | convolution fusion | flops 3246915584 | bytes 8921096 | tf_op jit(solution)/shard_map/dot_general | solution.py:93
  196.9 0.0 copy-done
  (2 shorter events, 0.0 us)
Async XLA Ops:
  9.8 30.7 %all-to-all-start = ((f32[4,256,512]{1,2,0:T(8,128)}), f32[4,256,512]{1,2,0:T(8,128)S(1)}, u32[]{:S(2)}, u32[]{:S(2)}) async-start(f32[4,256,512]{1,2,0:T(8,128)} %bitcast.30), calls=%async_computation | async-start | bytes 4194304 | tf_op jit(solution)/shard_map/all_to_all | solution.py:18
  40.5 52.8 %all-to-all-start.2 = ((bf16[256,4,2048]{0,2,1:T(8,128)(2,1)}), bf16[256,4,2048]{0,2,1:T(8,128)(2,1)}, u32[]{:S(2)}, u32[]{:S(2)}) async-start(bf16[256,4,2048]{0,2,1:T(8,128)(2,1)} %bitcast.27), calls=%async_computation.2 | async-start | bytes 8388608 | tf_op jit(solution)/shard_map/all_to_all | solution.py:85
  94.4 16.7 %all-to-all-start.1 = ((bf16[4,256,512]{2,1,0:T(8,128)(2,1)}), bf16[4,256,512]{2,1,0:T(8,128)(2,1)S(1)}, u32[]{:S(2)}, u32[]{:S(2)}) async-start(bf16[4,256,512]{2,1,0:T(8,128)(2,1)} %broadcast_in_dim.8), calls=%async_computation.1 | async-start | bytes 2097152 | tf_op jit(solution)/shard_map/all_to_all | solution.py:24
  136.8 38.5 %copy-start.1 = (f32[64,512]{1,0:T(8,128)S(1)}, f32[64,512]{1,0:T(8,128)}, u32[]{:S(2)}) copy-start(f32[64,512]{1,0:T(8,128)} %param.11) | copy-start | bytes 393220
  175.4 21.6 %copy-start = (f32[64,512]{1,0:T(8,128)}, f32[64,512]{1,0:T(8,128)S(1)}, u32[]{:S(2)}) copy-start(f32[64,512]{1,0:T(8,128)S(1)} %multiply_add_fusion.1) | copy-start | bytes 393220
where the time goes:
time: 198 us; the launch traced here: 197 us
  waiting for transfers between devices  69.8 us (35%)
  blocking collectives  56 us (28%)
  local copies, waits for them, and re-layouts  28.3 us (14%)
  matrix products  23.3 us (12%)
  starting transfers between devices  12.8 us (6%)
  other arithmetic  4.8 us (2%)
  between operations  2.03 us (1%)
    all_to_all x1, waiting for transfers between devices, per_device(): lax.all_to_all(grouped, 'col', split_axis=1, concat_axis=0, tiled=True)  47.6 us
    all_to_all x1, blocking collectives, sum_in_two_steps(): return jnp.sum(lax.all_to_all(own, far, 0, 0, tiled=True), axis=0)  36.8 us
    all_to_all x1, waiting for transfers between devices, sent_and_summed(): pieces = lax.all_to_all(split_up(x, dim, count), axis, 0, 0, tiled=True)  15.2 us
    all_to_all x1, blocking collectives, from_everyone(): return lax.all_to_all(copies, axis, split_axis=0, concat_axis=0, tiled=True)  11.1 us
    dot_general x1, matrix products, per_device(): lax.dot_general(row_block, sign_block, (((1,), (1,)), ((), ())), precisio...  10.4 us
    all_to_all x1, blocking collectives, sent_and_summed(): pieces = lax.all_to_all(split_up(x, dim, count), axis, 0, 0, tiled=True)  8.17 us
    all_to_all x1, waiting for transfers between devices, from_everyone(): return lax.all_to_all(copies, axis, split_axis=0, concat_axis=0, tiled=True)  6.95 us
    dot_general x1, matrix products, contract(): lax.dot_general(left_rows, right_rows, (((0,), (0,)), ((), ())), preferre...  6.5 us
  transfers between devices with their start and end apart: 3, of which 3 were waited for; matrix products, arithmetic and copies ran while one was open for 9% of the time, Pallas kernels for 0%

commit v1 on v0

--- a/solution.py
+++ b/solution.py
@@ -82,7 +82,9 @@
     grouped = jnp.transpose(grouped, (0, 2, 1, 3)).reshape(
         quarter_rows, col_count, data_count * owner_rows
     )
-    regrouped = lax.all_to_all(grouped, "col", split_axis=1, concat_axis=0, tiled=True)
+    cells = jnp.split(grouped, lax.axis_size("col"), axis=1)
+    received = lax.all_to_all(jnp.stack(cells), "col", 0, 0)
+    regrouped = jnp.concatenate(received, axis=0)
     regrouped = regrouped.reshape(quarter_rows * col_count, data_count * owner_rows)
     shard_sketch = gather_directly(sketch, "col", 0)
     projected = sum_in_two_steps(contract(regrouped, shard_sketch), (("dp_0", "dp_1"), "dp_2"), 0)

time: 198 us -> 190 us (0.960)
  waiting for transfers between devices: 69.8 us -> 63 us
  local copies, waits for them, and re-layouts: 28.3 us -> 25.4 us
  other arithmetic: 4.8 us -> 7.05 us
  matrix products: 23.3 us -> 21.3 us
    all_to_all x1, waiting for transfers between devices: 6.95 us -> 0.44 us  [from_everyone(): return lax.all_to_all(copies, axis, split_axis=0, concat_axis=0, tiled=True)]
    another operation x0 -> x1, other arithmetic: none -> 2.25 us  [per_device(): received = lax.all_to_all(jnp.stack(cells), 'col', 0, 0)]
    transpose x1, local copies, waits for them, and re-layouts: 4.74 us -> 2.49 us  [per_device(): jnp.transpose(grouped, (0, 2, 1, 3))]
    transpose x1, local copies, waits for them, and re-layouts: 2.75 us -> 0.7 us  [split_up(): return jnp.moveaxis(x.reshape(*before, count, -1, *after), dim, 0)]
  transfers between devices with their start and end apart: 3 -> 3, of which waited for: 3 -> 3; matrix products, arithmetic and copies ran while one was open for 9% -> 13% of each run, Pallas kernels for 0% -> 0%
where the time goes in v1:
time: 190 us; the launch traced here: 189 us
  waiting for transfers between devices  63 us (33%)
  blocking collectives  57.4 us (30%)
  local copies, waits for them, and re-layouts  25.4 us (13%)
  matrix products  21.3 us (11%)
  starting transfers between devices  12.7 us (7%)
  other arithmetic  7.05 us (4%)
  between operations  2.05 us (1%)
    all_to_all x1, waiting for transfers between devices, per_device(): received = lax.all_to_all(jnp.stack(cells), 'col', 0, 0)  47.7 us
    all_to_all x1, blocking collectives, sum_in_two_steps(): return jnp.sum(lax.all_to_all(own, far, 0, 0, tiled=True), axis=0)  36.8 us
    all_to_all x1, waiting for transfers between devices, sent_and_summed(): pieces = lax.all_to_all(split_up(x, dim, count), axis, 0, 0, tiled=True)  14.9 us
    all_to_all x1, blocking collectives, from_everyone(): return lax.all_to_all(copies, axis, split_axis=0, concat_axis=0, tiled=True)  12.5 us
    dot_general x1, matrix products, per_device(): lax.dot_general(row_block, sign_block, (((1,), (1,)), ((), ())), precisio...  10.4 us
    all_to_all x1, blocking collectives, sent_and_summed(): pieces = lax.all_to_all(split_up(x, dim, count), axis, 0, 0, tiled=True)  8.16 us
    unnamed x5, local copies, waits for them, and re-layouts  6.4 us
    all_to_all x1, local copies, waits for them, and re-layouts, per_device(): received = lax.all_to_all(jnp.stack(cells), 'col', 0, 0)  6.4 us
  transfers between devices with their start and end apart: 3, of which 3 were waited for; matrix products, arithmetic and copies ran while one was open for 13% of the time, Pallas kernels for 0%

profile of v1, /device:TPU:0, one launch (start us, length us, event | category | flops | bytes accessed | tf_op | source)
XLA Modules:
  0.0 189.0 jit_solution(401841918610471110)
XLA Ops:
  1.9 6.4 %fusion.3 = f32[512,1024]{1,0:T(8,128)S(1)} fusion(bf16[1024,2048]{1,0:T(8,128)(2,1)} %param.7, s32[]{:T(128)} %bitcast.11, s32[]{:T(128)} %bitcast.10, s32[2048]{0:T(1024)S(1)} %add_multiply_fusion), kind=kOutput, calls=%fused_computation.10 | convolution fusion | flops 2170028032 | bytes 6299656 | tf_op jit(solution)/shard_map/dot_general | solution.py:72
  8.3 1.5 copy.48
  9.8 4.4 %all-to-all-start.1 = ((f32[4,256,512]{1,2,0:T(8,128)}), f32[4,256,512]{1,2,0:T(8,128)S(1)}, u32[]{:S(2)}, u32[]{:S(2)}) async-start(f32[4,256,512]{1,2,0:T(8,128)} %bitcast.38), calls=%async_computation.1 | async-start | bytes 4194304 | tf_op jit(solution)/shard_map/all_to_all | solution.py:18
  14.2 6.4 %copy.33 = bf16[256,8192]{0,1:T(8,128)(2,1)} copy(bf16[256,8192]{1,0:T(8,128)(2,1)} %param.8) | data formatting | bytes 8388608 | tf_op args[1]
  20.6 2.5 %copy.34 = bf16[256,4,32,64]{0,3,2,1:T(8,128)(2,1)S(1)} copy(bf16[256,4,32,64]{0,3,1,2:T(8,128)(2,1)} %bitcast.37) | data formatting | bytes 8388608 | tf_op jit(solution)/shard_map/transpose | solution.py:82
  23.1 0.3 slice_bitcast_fusion.3
  23.4 2.2 %pad_maximum_fusion = bf16[4,256,1,2048]{1,3,2,0:T(8,128)(2,1)} fusion(bf16[1,256,1,2048]{1,3,2,0:T(8,128)(2,1)S(1)} %get-tuple-element.6, bf16[1,256,1,2048]{1,3,2,0:T(8,128)(2,1)S(1)} %get-tuple-element.7, bf16[1,256,1,2048]{1,3,2,0:T(8,128)(2,1)S(1)} %get-tuple-element.8, bf16[1,256,1,2048]{1,3,2,0:T(8,128)(2,1)S(1)} %get-tuple-element.5), kind=kLoop, calls=%fused_computation | loop fusion | flops 6291456 | bytes 8388608 | tf_op jit(solution)/shard_map/stack | solution.py:86
  25.6 14.9 %all-to-all-done.1 = f32[4,256,512]{1,2,0:T(8,128)S(1)} async-done(((f32[4,256,512]{1,2,0:T(8,128)}), f32[4,256,512]{1,2,0:T(8,128)S(1)}, u32[]{:S(2)}, u32[]{:S(2)}) %all-to-all-start.1) | async-done | bytes 2097184 | tf_op jit(solution)/shard_map/all_to_all | solution.py:18
  40.5 4.8 %all-to-all-start = ((bf16[4,256,1,2048]{1,3,2,0:T(8,128)(2,1)}), bf16[4,256,1,2048]{1,3,2,0:T(8,128)(2,1)}, u32[]{:S(2)}, u32[]{:S(2)}) async-start(bf16[4,256,1,2048]{1,3,2,0:T(8,128)(2,1)} %pad_maximum_fusion), calls=%async_computation | async-start | bytes 8388608 | tf_op jit(solution)/shard_map/all_to_all | solution.py:86
  45.4 0.1 reduce_sum.27
  45.5 0.1 copy.41
  45.7 47.7 %all-to-all-done = bf16[4,256,1,2048]{1,3,2,0:T(8,128)(2,1)} async-done(((bf16[4,256,1,2048]{1,3,2,0:T(8,128)(2,1)}), bf16[4,256,1,2048]{1,3,2,0:T(8,128)(2,1)}, u32[]{:S(2)}, u32[]{:S(2)}) %all-to-all-start) | async-done | bytes 4194336 | tf_op jit(solution)/shard_map/all_to_all | solution.py:86
  93.3 1.1 broadcast_in_dim.8
  94.4 3.5 %all-to-all-start.2 = ((bf16[4,256,512]{2,1,0:T(8,128)(2,1)}), bf16[4,256,512]{2,1,0:T(8,128)(2,1)S(1)}, u32[]{:S(2)}, u32[]{:S(2)}) async-start(bf16[4,256,512]{2,1,0:T(8,128)(2,1)} %broadcast_in_dim.8), calls=%async_computation.2 | async-start | bytes 2097152 | tf_op jit(solution)/shard_map/all_to_all | solution.py:24
  97.9 6.4 %copy.37 = bf16[4,256,1,2048]{3,1,0,2:T(8,128)(2,1)} copy(bf16[4,256,1,2048]{1,3,2,0:T(8,128)(2,1)} %all-to-all-done) | data formatting | bytes 8388608 | tf_op jit(solution)/shard_map/all_to_all | solution.py:86
  104.3 6.4 %copy.38 = bf16[2048,1024]{1,0:T(8,128)(2,1)} copy(bf16[2048,1024]{0,1:T(8,128)(2,1)} %bitcast.36) | data formatting | bytes 8388608 | tf_op jit(solution)/shard_map/dot_general | solution.py:59
  110.7 0.4 all-to-all-done.2
  111.1 4.5 %convolution_bitcast_fusion = f32[2,16,64,512]{3,2,0,1:T(8,128)S(1)} fusion(bf16[16,2,64,1024]{3,2,1,0:T(8,128)(2,1)} %bitcast.39, bf16[1024,512,1,1]{1,0,3,2:T(8,128)(2,1)S(1)} %bitcast.41), kind=kOutput, calls=%fused_computation.5 | convolution fusion | flops 2147483648 | bytes 9437184 | tf_op jit(solution)/shard_map/dot_general | solution.py:59
  115.7 0.7 copy.42
  116.4 8.2 %all_to_all.30 = f32[2,16,64,512]{3,2,1,0:T(8,128)} all-to-all(f32[2,16,64,512]{3,2,1,0:T(8,128)S(1)} %copy.42), channel_id=1, replica_groups=mesh['dp_0'=4,'dp_1'=4,'dp_2'=2,'col'=4] {'dp_2'}, dimensions={0} | all-to-all | bytes 8388608 | tf_op jit(solution)/shard_map/all_to_all | solution.py:18
  124.5 2.9 %reduce_sum.28 = f32[16,64,512]{2,1,0:T(8,128)S(1)} reduce(f32[2,16,64,512]{3,2,1,0:T(8,128)} %all_to_all.30, f32[]{:T(128)} %constant.21.clone.1), dimensions={0}, to_apply=%region_1.0 | reduce | flops 524288 | bytes 6291460 | tf_op jit(solution)/shard_map/reduce_sum | solution.py:19
  127.4 0.0 copy-start.1
  127.4 36.8 %all_to_all.31 = f32[16,64,512]{2,1,0:T(8,128)} all-to-all(f32[16,64,512]{2,1,0:T(8,128)S(1)} %reduce_sum.28), channel_id=1, replica_groups=mesh['dp_0'=4,'dp_1'=4,'dp_2'=2,'col'=4] {'dp_0','dp_1'}, dimensions={0} | all-to-all | bytes 4194304 | tf_op jit(solution)/shard_map/all_to_all | solution.py:41
  164.2 1.8 reduce_sum.29
  166.0 0.0 copy-done.1
  166.0 0.0 copy-start
  166.0 0.1 broadcast_in_dim.9
  166.1 12.5 %all_to_all.32 = f32[4,64,512]{2,1,0:T(8,128)S(1)} all-to-all(f32[4,64,512]{2,1,0:T(8,128)S(1)} %broadcast_in_dim.9), channel_id=1, replica_groups=mesh['dp_0'=4,'dp_1'=4,'dp_2'=2,'col'=4] {'col'}, dimensions={0} | all-to-all | bytes 1048576 | tf_op jit(solution)/shard_map/all_to_all | solution.py:24
  178.6 10.4 %divide_subtract_fusion = (f32[256,2048]{1,0:T(8,128)}, f32[256,2048]{1,0:T(8,128)}) fusion(f32[256,2048]{1,0:T(8,128)} %param.9, f32[256,2048]{1,0:T(8,128)} %param.10, f32[256,512]{1,0:T(8,128)S(1)} %bitcast.42, s32[]{:T(128)} %bitcast.11, s32[]{:T(128)} %bitcast.10, s32[2048]{0:T(1024)S(1)} %add_multiply_fusion), kind=kOutput, calls=%fused_computation.8 | convolution fusion | flops 3246915584 | bytes 8921096 | tf_op jit(solution)/shard_map/dot_general | solution.py:95
  189.0 0.0 copy-done
  (2 shorter events, 0.0 us)
Async XLA Ops:
  9.8 30.7 %all-to-all-start.1 = ((f32[4,256,512]{1,2,0:T(8,128)}), f32[4,256,512]{1,2,0:T(8,128)S(1)}, u32[]{:S(2)}, u32[]{:S(2)}) async-start(f32[4,256,512]{1,2,0:T(8,128)} %bitcast.38), calls=%async_computation.1 | async-start | bytes 4194304 | tf_op jit(solution)/shard_map/all_to_all | solution.py:18
  40.5 52.8 %all-to-all-start = ((bf16[4,256,1,2048]{1,3,2,0:T(8,128)(2,1)}), bf16[4,256,1,2048]{1,3,2,0:T(8,128)(2,1)}, u32[]{:S(2)}, u32[]{:S(2)}) async-start(bf16[4,256,1,2048]{1,3,2,0:T(8,128)(2,1)} %pad_maximum_fusion), calls=%async_computation | async-start | bytes 8388608 | tf_op jit(solution)/shard_map/all_to_all | solution.py:86
  94.4 16.8 %all-to-all-start.2 = ((bf16[4,256,512]{2,1,0:T(8,128)(2,1)}), bf16[4,256,512]{2,1,0:T(8,128)(2,1)S(1)}, u32[]{:S(2)}, u32[]{:S(2)}) async-start(bf16[4,256,512]{2,1,0:T(8,128)(2,1)} %broadcast_in_dim.8), calls=%async_computation.2 | async-start | bytes 2097152 | tf_op jit(solution)/shard_map/all_to_all | solution.py:24
  127.4 38.5 %copy-start.1 = (f32[64,512]{1,0:T(8,128)S(1)}, f32[64,512]{1,0:T(8,128)}, u32[]{:S(2)}) copy-start(f32[64,512]{1,0:T(8,128)} %param.11) | copy-start | bytes 393220
  166.0 23.0 %copy-start = (f32[64,512]{1,0:T(8,128)}, f32[64,512]{1,0:T(8,128)S(1)}, u32[]{:S(2)}) copy-start(f32[64,512]{1,0:T(8,128)S(1)} %multiply_add_fusion.1) | copy-start | bytes 393220
